TPU v7x, 256 devices: a whole 4x4x8 slice. The times are simulated.
256 devices in a mesh: req: 64 (over y, z, core), mlp: 4 (over x).
Axes of the slice: x: 4, y: 4, z: 8, core: 2. Of those that a mesh axis runs over, the one named last changes fastest.
Arguments:
- queries: bfloat16 [64, 2, 16, 2, 1536], P('req', None, 'mlp'), may hold values from -64 to 64
- new_kv: bfloat16 [64, 2, 16, 2, 256], P('req', None, 'mlp'), may hold values from -9 to 9
- residual: bfloat16 [64, 2, 16, 2, 1536], P('req', None, 'mlp'), may hold values from -3 to 3
- prompt_kv: bfloat16 [64, 1024, 256], P('req'), may hold values from -9 to 9
- tail_kv: bfloat16 [64, 16, 64, 256], P('req', 'mlp'), may hold values from -9 to 9
- page_pool: bfloat16 [16384, 20, 256], P(('req', 'mlp')), may hold values from -9 to 9
- page_holder: int32 [256, 64], P(('req', 'mlp')), may hold values from 0 to 63, as said below
- serve_slot: int32 [256, 64], P(('req', 'mlp')), may hold values from 0 to 63
- prompt_len: int32 [64, 2], P('req'), may hold values from 512 to 32768
- tail_len: int32 [64, 2, 16], P('req', None, 'mlp'), may hold values from 1 to 62, 496 in all within a row
- w_out: bfloat16 [1536, 1536], P('mlp'), may hold values from -0.15625 to 0.15625
- norm_mlp: float32 [1536], replicated, may hold values from 0.25 to 1.75
- w_gate: bfloat16 [1536, 4608], P(None, 'mlp'), may hold values from -0.15625 to 0.15625
- w_up: bfloat16 [1536, 4608], P(None, 'mlp'), may hold values from -0.15625 to 0.15625
- w_down: bfloat16 [4608, 1536], P('mlp'), may hold values from -0.09375 to 0.09375
- norm_final: float32 [1536], replicated, may hold values from 0.25 to 1.75
- w_score: float32 [1536], replicated, may hold values from -0.15625 to 0.15625
Outputs:
- scores: float32 [64, 2, 16, 2], P('req', None, 'mlp')
- hidden_out: bfloat16 [64, 2, 16, 2, 1536], P('req', None, 'mlp')
- tails_out: bfloat16 [64, 2, 16, 64, 256], P('req', None, 'mlp')
Inputs may be any that keep to these rules, and one draw needn't show every extreme that they name: Each row of page_holder names every req index once.
All inputs are finite; a program needn't handle non-finite values. No bound on the sum of `tail_len` on one device may be relied on, other than what follows from the above.
Results may differ from a plain program's by a relative error of at most 0.015.
Values may be sent and summed in bfloat16 or wider, within the bound.
No kernel may reach another device: no remote copies, remote signals or barrier semaphores. Data moves between devices by JAX's collectives and lax.ppermute only.
A program may use at most 64 MiB of HBM per device.

v0:
```python
import jax
import jax.numpy as jnp
from jax import lax
from jax.sharding import PartitionSpec as P


def attend(query, fresh, window, tails, plen, tlen):
    count = query.shape[0]
    size = window.shape[-1] // 2
    q = query.reshape(count, 2, -1, size)
    scale = 1.0 / jnp.sqrt(jnp.float32(size))
    s_win = (
        jnp.einsum("sthd,kd->sthk", q, window[:, :size], preferred_element_type=jnp.float32) * scale
    )
    s_tail = (
        jnp.einsum("sthd,sjd->sthj", q, tails[..., :size], preferred_element_type=jnp.float32)
        * scale
    )
    s_new = (
        jnp.einsum("sthd,sud->sthu", q, fresh[..., :size], preferred_element_type=jnp.float32)
        * scale
    )
    tpos = tlen[:, None] + jnp.arange(2, dtype=jnp.int32)[None, :]
    kw = jnp.arange(window.shape[0], dtype=jnp.int32)[None, None, None, :]
    ok_win = (kw >= window.shape[0] - plen) & (kw > tpos[:, :, None, None])
    kt = jnp.arange(tails.shape[1], dtype=jnp.int32)[None, None, None, :]
    ok_tail = kt < tlen[:, None, None, None]
    steps = jnp.arange(2, dtype=jnp.int32)
    ok_new = steps[None, None, None, :] <= steps[None, :, None, None]
    s_win = jnp.where(ok_win, s_win, -1e30)
    s_tail = jnp.where(ok_tail, s_tail, -1e30)
    s_new = jnp.where(ok_new, s_new, -1e30)
    top = jnp.maximum(jnp.maximum(s_win.max(-1), s_tail.max(-1)), s_new.max(-1))[..., None]
    e_win = jnp.where(ok_win, jnp.exp(s_win - top), 0.0)
    e_tail = jnp.where(ok_tail, jnp.exp(s_tail - top), 0.0)
    e_new = jnp.where(ok_new, jnp.exp(s_new - top), 0.0)
    total = (
        e_win.sum(-1, keepdims=True) + e_tail.sum(-1, keepdims=True) + e_new.sum(-1, keepdims=True)
    )
    p_win = (e_win / total).astype(jnp.bfloat16)
    p_tail = (e_tail / total).astype(jnp.bfloat16)
    p_new = (e_new / total).astype(jnp.bfloat16)
    out = jnp.einsum("sthk,kd->sthd", p_win, window[:, size:], preferred_element_type=jnp.float32)
    out = out + jnp.einsum(
        "sthj,sjd->sthd", p_tail, tails[..., size:], preferred_element_type=jnp.float32
    )
    out = out + jnp.einsum(
        "sthu,sud->sthd", p_new, fresh[..., size:], preferred_element_type=jnp.float32
    )
    return out.reshape(count, 2, -1).astype(jnp.bfloat16)


def extend(tails, fresh, tlen):
    rows = jnp.arange(tails.shape[1], dtype=jnp.int32)[None, :, None]
    lead = tlen[:, None, None]
    out = jnp.where(rows == lead, fresh[:, 0][:, None, :], tails)
    return jnp.where(rows == lead + 1, fresh[:, 1][:, None, :], out)


def rms_scale(values):
    return values * lax.rsqrt(jnp.mean(values * values, axis=-1, keepdims=True) + 1e-06)


def on_device(
    queries,
    new_kv,
    residual,
    prompt_kv,
    tail_kv,
    page_pool,
    page_holder,
    serve_slot,
    prompt_len,
    tail_len,
    w_out,
    norm_mlp,
    w_gate,
    w_up,
    w_down,
    norm_final,
    w_score,
):
    samp_dev = queries.shape[2]
    width = residual.shape[-1]
    kv_width = new_kv.shape[-1]
    win_rows = prompt_kv.shape[1]
    tail_rows = tail_kv.shape[2]
    outgoing = jnp.take(page_pool, serve_slot[0], axis=0)
    arrived = lax.all_to_all(outgoing, "req", split_axis=0, concat_axis=0, tiled=True)
    fetched = jnp.take(arrived, page_holder[0], axis=0).reshape(-1, kv_width)
    moved_window = fetched[:win_rows]
    moved_tails = fetched[win_rows:].reshape(samp_dev, tail_rows, kv_width)
    first = attend(
        queries[0, 0], new_kv[0, 0], prompt_kv[0], tail_kv[0], prompt_len[0, 0], tail_len[0, 0]
    )
    second = attend(
        queries[0, 1], new_kv[0, 1], moved_window, moved_tails, prompt_len[0, 1], tail_len[0, 1]
    )
    attn = jnp.stack([first, second])[None]
    tails_out = jnp.stack(
        [
            extend(tail_kv[0], new_kv[0, 0], tail_len[0, 0]),
            extend(moved_tails, new_kv[0, 1], tail_len[0, 1]),
        ]
    )[None]
    block_width = w_out.shape[0]
    position = lax.axis_index("mlp")
    every = lax.all_gather(attn, "mlp", axis=2, tiled=True)
    block = lax.dynamic_slice_in_dim(every, position * block_width, block_width, 4)
    partial_sum = jnp.dot(block.reshape(-1, block_width), w_out, preferred_element_type=jnp.float32)
    mixed = lax.psum(partial_sum, "mlp")
    res_all = lax.all_gather(residual, "mlp", axis=2, tiled=True).reshape(-1, width)
    h1_all = (res_all.astype(jnp.float32) + mixed).astype(jnp.bfloat16)
    h1_own = lax.dynamic_slice_in_dim(
        h1_all.reshape(2, -1, 2, width), position * samp_dev, samp_dev, 1
    )
    normed = (rms_scale(h1_all.astype(jnp.float32)) * norm_mlp).astype(jnp.bfloat16)
    gate = jnp.dot(normed, w_gate, preferred_element_type=jnp.float32)
    up = jnp.dot(normed, w_up, preferred_element_type=jnp.float32)
    act = (jax.nn.gelu(gate, approximate=True) * up).astype(jnp.bfloat16)
    down_terms = jnp.dot(act, w_down, preferred_element_type=jnp.float32).reshape(2, -1, 2, width)
    down_own = lax.psum_scatter(
        down_terms.astype(jnp.bfloat16), "mlp", scatter_dimension=1, tiled=True
    ).astype(jnp.float32)
    h2 = h1_own.astype(jnp.float32) + down_own
    scores = jnp.sum(rms_scale(h2) * norm_final * w_score, axis=-1)
    return (scores[None], h2.astype(jnp.bfloat16)[None], tails_out)


def solution(mesh):
    placed = (
        P("req", None, "mlp", None, None),
        P("req", None, "mlp", None, None),
        P("req", None, "mlp", None, None),
        P("req", None, None),
        P("req", "mlp", None, None),
        P(("req", "mlp"), None, None),
        P(("req", "mlp"), None),
        P(("req", "mlp"), None),
        P("req", None),
        P("req", None, "mlp"),
        P("mlp", None),
        P(),
        P(None, "mlp"),
        P(None, "mlp"),
        P("mlp", None),
        P(),
        P(),
    )
    return jax.shard_map(
        on_device,
        mesh=mesh,
        in_specs=placed,
        out_specs=(
            P("req", None, "mlp", None),
            P("req", None, "mlp", None, None),
            P("req", None, "mlp", None, None),
        ),
        check_vma=False,
    )
```

profile of v0, /device:TPU:8, one launch (start us, length us, event | category | flops | bytes accessed | tf_op | source)
XLA Modules:
  0.0 237.5 jit_solution(120826959070692707)
XLA Ops:
  7.2 0.8 compare_select_fusion.1
  8.0 1.3 compare_and_fusion.3
  9.3 3.8 %gather_fusion = bf16[64,20,256]{2,0,1:T(8,128)(2,1)} fusion(bf16[64,20,256]{2,0,1:T(8,128)(2,1)} %param.24, s32[1024]{0:T(1024)S(1)} %pad_clamp_fusion.1), kind=kCustom, calls=%fused_computation.clone | custom fusion | bytes 1310976 | tf_op jit(solution)/shard_map/jit(_take)/gather | solution.py:88
  13.1 1.3 broadcast_select_fusion.1
  14.4 1.3 copy.22
  15.7 12.3 %all-to-all-start = ((bf16[64,20,256]{2,1,0:T(8,128)(2,1)}), bf16[64,20,256]{2,1,0:T(8,128)(2,1)}, u32[]{:S(2)}, u32[]{:S(2)}) async-start(bf16[64,20,256]{2,1,0:T(8,128)(2,1)} %copy.22), calls=%async_computation | async-start | bytes 1572864 | tf_op jit(solution)/shard_map/all_to_all | solution.py:89
  31.1 1.4 fusion.62
  34.4 1.4 reshape_squeeze.6
  36.9 1.6 fusion.66
  38.5 1.1 fusion.68
  39.6 0.8 compare_and_fusion.1
  40.4 2.0 fusion.67
  42.4 1.3 fusion.32
  43.8 14.0 %all_gather.6 = bf16[1,2,16,2,1536]{4,3,2,1,0:T(2,128)(2,1)} all-gather(bf16[1,2,4,2,1536]{4,3,2,1,0:T(2,128)(2,1)} %param.21), channel_id=1, replica_groups=mesh['req'=64,'mlp'=4] {'mlp'}, dimensions={2}, use_global_device_ids=true | all-gather | bytes 245760 | tf_op jit(solution)/shard_map/all_gather | solution.py:112
  57.8 1.4 reshape_squeeze.7
  59.2 1.7 reshape.390
  60.9 1.3 copy.46
  62.2 1.3 copy.47
  63.5 1.3 copy.48
  64.7 1.3 copy.49
  66.0 1.3 dynamic-slice.1
  67.9 1.9 fusion.11
  69.8 1.2 compare_and_fusion.2
  71.0 1.3 broadcast_add_fusion.1
  72.2 0.7 iota_add_fusion
  72.9 1.4 compare_and_fusion
  74.3 2.1 fusion.69
  76.4 2.8 %gather_fusion.1 = bf16[64,20,256]{2,1,0:T(8,128)(2,1)} fusion(bf16[64,20,256]{2,1,0:T(8,128)(2,1)} %all-to-all-done, s32[1024]{0:T(1024)} %pad_clamp_fusion), kind=kCustom, calls=%fused_computation.1.clone | custom fusion | bytes 1310976 | tf_op jit(solution)/shard_map/jit(_take)/gather | solution.py:90
  79.2 2.2 broadcast_select_fusion
  81.4 2.0 reshape.385
  83.4 1.0 slice.118
  84.4 2.1 fusion.70
  86.5 1.5 fusion.71
  88.0 0.7 maximum_maximum_fusion
  89.3 1.4 fusion.50
  90.7 0.7 add_add_fusion.1
  91.4 1.4 fusion.25
  93.1 0.9 fusion.7
  94.0 1.4 convert_element_type.83
  95.4 1.0 fusion.33
  96.4 1.3 fusion.12
  97.7 0.7 add_add_fusion
  98.4 1.5 fusion.24
  99.9 1.1 convolution_add_fusion.1
  101.0 1.6 fusion.8
  102.6 1.4 convert_element_type.88
  103.9 0.8 pad_maximum_fusion
  104.8 12.1 %all-gather = bf16[2,16,2,1536]{3,2,1,0:T(2,128)(2,1)S(1)} all-gather(bf16[2,4,2,1536]{3,2,1,0:T(2,128)(2,1)S(1)} %pad_maximum_fusion), channel_id=2, replica_groups=mesh['req'=64,'mlp'=4] {'mlp'}, dimensions={1}, use_global_device_ids=true | all-gather | bytes 245760 | tf_op jit(solution)/shard_map/all_gather | solution.py:108
  117.6 1.4 reshape.387
  119.0 2.4 %fusion.72 = f32[64,1536]{1,0:T(8,128)} fusion(bf16[64,384]{1,0:T(8,128)(2,1)} %reshape.387, bf16[384,1536]{1,0:T(8,128)(2,1)} %param.29), kind=kOutput, calls=%fused_computation.155 | convolution fusion | flops 75497472 | bytes 1622016 | tf_op jit(solution)/shard_map/dot_general | solution.py:110
  121.4 1.3 iota_compare_fusion.3
  122.7 1.7 select_select_fusion.1
  124.4 44.4 %all-reduce.4.cloned.1.call-done = f32[64,1536]{1,0:T(8,128)} async-done(((f32[64,1536]{1,0:T(8,128)}), f32[64,1536]{1,0:T(8,128)}) %all-reduce.4.cloned.1.call-update) | async-done | bytes 393232 | tf_op jit(solution)/shard_map/psum | solution.py:111
  168.8 1.3 fusion.13
  170.7 3.5 %fusion.36 = f32[64,1152]{1,0:T(8,128)} fusion(bf16[1536,1152]{1,0:T(8,128)(2,1)} %param.31, bf16[64,1536]{1,0:T(8,128)(2,1)S(1)} %get-tuple-element.7, f32[1536]{0:T(1024)S(1)} %copy-done.14, f32[64]{0:T(128)S(1)} %add_rsqrt_fusion.1), kind=kOutput, calls=%fused_computation.77 | convolution fusion | flops 226885632 | bytes 4036864 | tf_op jit(solution)/shard_map/dot_general | solution.py:118
  174.2 4.2 %convolution_convert_fusion = bf16[64,1536]{1,0:T(8,128)(2,1)} fusion(bf16[1152,1536]{1,0:T(8,128)(2,1)S(1)} %copy-done, bf16[1536,1152]{1,0:T(8,128)(2,1)} %param.32, f32[64,1152]{1,0:T(8,128)} %fusion.36, bf16[64,1536]{1,0:T(8,128)(2,1)} %copy-done.1, f32[1536]{0:T(1024)S(1)} %copy-done.14, f32[64]{0:T(128)} %copy-done.22), kind=kOutput, calls=%fused_computation.4 | convolution fusion | flops 454213632 | bytes 7772416 | tf_op jit(solution)/shard_map/dot_general | solution.py:121
  178.4 1.7 convert_element_type.95
  180.2 1.0 select_select_fusion
  181.2 1.6 maximum_bitcast_fusion
  182.9 1.7 reshape.388
  184.5 42.9 %all-reduce.6.cloned.1.call-done = bf16[2,16,2,1536]{3,2,1,0:T(2,128)(2,1)} async-done(((bf16[2,16,2,1536]{3,2,1,0:T(2,128)(2,1)}), bf16[2,16,2,1536]{3,2,1,0:T(2,128)(2,1)}) %all-reduce.6.cloned.1.call-update) | async-done | bytes 196624
  227.4 1.0 multiply_reduce_fusion.1
  228.4 1.5 fusion.39
  229.9 0.7 copy.23
  (72 shorter events, 7.2 us)
Async XLA Ops:
  7.2 167.0 %copy-start = (bf16[1152,1536]{1,0:T(8,128)(2,1)S(1)}, bf16[1152,1536]{1,0:T(8,128)(2,1)}, u32[]{:S(2)}) copy-start(bf16[1152,1536]{1,0:T(8,128)(2,1)} %param.33) | copy-start | bytes 10616836
  13.1 15.4 %copy-start.21 = (s32[1,2,4]{2,1,0:T(2,128)S(1)}, s32[1,2,4]{2,1,0:T(2,128)}, u32[]{:S(2)}) copy-start(s32[1,2,4]{2,1,0:T(2,128)} %param.28) | copy-start | bytes 100
  13.1 19.4 %copy-start.23 = (s32[1,2]{1,0:T(1,128)S(1)}, s32[1,2]{1,0:T(1,128)}, u32[]{:S(2)}) copy-start(s32[1,2]{1,0:T(1,128)} %param.27) | copy-start | bytes 28
  13.1 21.2 %copy-start.17 = (bf16[1,2,4,2,256]{4,3,2,1,0:T(2,128)(2,1)S(1)}, bf16[1,2,4,2,256]{4,3,2,1,0:T(2,128)(2,1)}, u32[]{:S(2)}) copy-start(bf16[1,2,4,2,256]{4,3,2,1,0:T(2,128)(2,1)} %param.20) | copy-start | bytes 24580
  15.7 60.7 %all-to-all-start = ((bf16[64,20,256]{2,1,0:T(8,128)(2,1)}), bf16[64,20,256]{2,1,0:T(8,128)(2,1)}, u32[]{:S(2)}, u32[]{:S(2)}) async-start(bf16[64,20,256]{2,1,0:T(8,128)(2,1)} %copy.22), calls=%async_computation | async-start | bytes 1572864 | tf_op jit(solution)/shard_map/all_to_all | solution.py:89
  28.0 140.8 %all-reduce.4.cloned.1.call-start = ((), (), s32[]{:S(2)}) async-start(), calls=%async_computation.1 | async-start | bytes 786432 | tf_op jit(solution)/shard_map/psum | solution.py:111
  28.5 5.8 %copy-start.20 = (s32[4]{0:T(128)}, s32[4]{0:T(128)S(1)}, u32[]{:S(2)}) copy-start(s32[4]{0:T(128)S(1)} %get-tuple-element.21) | copy-start | bytes 52
  34.3 4.2 %copy-start.10 = (bf16[4,2,256]{2,1,0:T(2,128)(2,1)}, bf16[4,2,256]{2,1,0:T(2,128)(2,1)S(1)}, u32[]{:S(2)}) copy-start(bf16[4,2,256]{2,1,0:T(2,128)(2,1)S(1)} %get-tuple-element.12) | copy-start | bytes 12292
  34.3 4.1 %copy-start.12 = (bf16[4,2,256]{2,1,0:T(2,128)(2,1)}, bf16[4,2,256]{2,1,0:T(2,128)(2,1)S(1)}, u32[]{:S(2)}) copy-start(bf16[4,2,256]{2,1,0:T(2,128)(2,1)S(1)} %get-tuple-element.13) | copy-start | bytes 12292
  39.6 2.9 %copy-start.4 = (f32[4,2,12,64]{3,2,1,0:T(8,128)}, f32[4,2,12,64]{3,2,1,0:T(8,128)S(1)}, u32[]{:S(2)}) copy-start(f32[4,2,12,64]{3,2,1,0:T(8,128)S(1)} %get-tuple-element.33) | copy-start | bytes 73732
  42.4 1.4 copy-start.6
  83.4 9.4 %copy-start.3 = (bf16[1,4,64,256]{3,2,1,0:T(8,128)(2,1)S(1)}, bf16[1,4,64,256]{3,2,1,0:T(8,128)(2,1)}, u32[]{:S(2)}) copy-start(bf16[1,4,64,256]{3,2,1,0:T(8,128)(2,1)} %param.23) | copy-start | bytes 393220
  83.4 9.4 %copy-start.5 = (f32[4,2,12,64]{3,2,1,0:T(8,128)S(1)}, f32[4,2,12,64]{3,2,1,0:T(8,128)}, u32[]{:S(2)}) copy-start(f32[4,2,12,64]{3,2,1,0:T(8,128)} %copy-done.4) | copy-start | bytes 73732
  83.4 9.5 %copy-start.7 = (f32[1,8,12]{2,1,0:T(8,128)S(1)}, f32[1,8,12]{2,1,0:T(8,128)}, u32[]{:S(2)}) copy-start(f32[1,8,12]{2,1,0:T(8,128)} %copy-done.6) | copy-start | bytes 1156
  83.4 9.5 %copy-start.19 = (pred[4,64]{1,0:T(4,128)(4,1)S(1)}, pred[4,64]{1,0:T(4,128)(4,1)}, u32[]{:S(2)}) copy-start(pred[4,64]{1,0:T(4,128)(4,1)} %get-tuple-element.40) | copy-start | bytes 772
  83.4 9.7 %copy-start.13 = (bf16[4,2,256]{2,1,0:T(2,128)(2,1)S(1)}, bf16[4,2,256]{2,1,0:T(2,128)(2,1)}, u32[]{:S(2)}) copy-start(bf16[4,2,256]{2,1,0:T(2,128)(2,1)} %copy-done.12) | copy-start | bytes 12292
  83.4 9.7 %copy-start.18 = (f32[4,2,12,2]{2,3,1,0:T(2,128)S(1)}, f32[4,2,12,2]{2,3,1,0:T(2,128)}, u32[]{:S(2)}) copy-start(f32[4,2,12,2]{2,3,1,0:T(2,128)} %get-tuple-element.29) | copy-start | bytes 2308
  83.4 9.7 %copy-start.24 = (pred[2,2]{1,0:T(4,128)(4,1)S(1)}, pred[2,2]{1,0:T(4,128)(4,1)}, u32[]{:S(2)}) copy-start(pred[2,2]{1,0:T(4,128)(4,1)} %iota_compare_fusion.8) | copy-start | bytes 16
  84.4 2.1 copy-start.2
  88.7 0.6 copy-start.8
  92.8 7.0 %copy-start.9 = (f32[1,8,12]{2,1,0:T(8,128)S(1)}, f32[1,8,12]{2,1,0:T(8,128)}, u32[]{:S(2)}) copy-start(f32[1,8,12]{2,1,0:T(8,128)} %copy-done.8) | copy-start | bytes 1156
  92.9 8.1 %copy-start.11 = (bf16[4,2,256]{2,1,0:T(2,128)(2,1)S(1)}, bf16[4,2,256]{2,1,0:T(2,128)(2,1)}, u32[]{:S(2)}) copy-start(bf16[4,2,256]{2,1,0:T(2,128)(2,1)} %copy-done.10) | copy-start | bytes 12292
  98.4 72.3 %copy-start.14 = (f32[1536]{0:T(1024)S(1)}, f32[1536]{0:T(1024)}, u32[]{:S(2)}) copy-start(f32[1536]{0:T(1024)} %param.30) | copy-start | bytes 18436
  121.4 106.0 %all-reduce.6.cloned.1.call-start = ((), (), s32[]{:S(2)}) async-start(), calls=%async_computation.2 | async-start | bytes 393216
  170.0 0.7 copy-start.1
  170.1 0.7 copy-start.22
  174.2 5.9 %copy-start.15 = (bf16[4,1,256]{2,0,1:T(4,128)(2,1)S(1)}, bf16[4,1,256]{2,0,1:T(4,128)(2,1)}, u32[]{:S(2)}) copy-start(bf16[4,1,256]{2,0,1:T(4,128)(2,1)} %copy.46) | copy-start | bytes 6148
  174.2 6.0 %copy-start.16 = (bf16[4,1,256]{2,0,1:T(4,128)(2,1)S(1)}, bf16[4,1,256]{2,0,1:T(4,128)(2,1)}, u32[]{:S(2)}) copy-start(bf16[4,1,256]{2,0,1:T(4,128)(2,1)} %copy.47) | copy-start | bytes 6148
Sparse Core Ops, SparseCore 0:
  121.5 47.1 all-reduce.3
  180.3 47.1 all-reduce.5
where the time goes:
time: 240 us; the launch traced here: 237 us
  waiting for transfers between devices  87.3 us (36%)
  local copies, waits for them, and re-layouts  34.4 us (14%)
  other arithmetic  33.8 us (14%)
  matrix products  27.1 us (11%)
  blocking collectives  26.2 us (11%)
  between operations  16.2 us (7%)
  starting transfers between devices  12.4 us (5%)
    psum x1, waiting for transfers between devices, on_device(): mixed = lax.psum(partial_sum, 'mlp')  44.4 us
    unnamed x3, waiting for transfers between devices  42.9 us
    all_gather x1, blocking collectives, on_device(): lax.all_gather(residual, 'mlp', axis=2, tiled=True).reshape(-1, width)  14 us
    all_to_all x1, starting transfers between devices, on_device(): lax.all_to_all(outgoing, 'req', split_axis=0, concat_axis=0, tiled=True)  12.3 us
    all_gather x1, blocking collectives, on_device(): every = lax.all_gather(attn, 'mlp', axis=2, tiled=True)  12.1 us
    unnamed x56, local copies, waits for them, and re-layouts  8.28 us
  transfers between devices with their start and end apart: 3, of which 2 were waited for; matrix products, arithmetic and copies ran while one was open for 17% of the time, Pallas kernels for 0%

commit v1 on v0

--- a/solution.py
+++ b/solution.py
@@ -1,7 +1,16 @@
+import functools
 import jax
 import jax.numpy as jnp
 from jax import lax
 from jax.sharding import PartitionSpec as P
+
+
+def show_state(mine, mesh_name):
+    last = lax.all_gather(mine, axis_name=mesh_name).sum(axis=0)
+    return last
+
+
+region_match = functools.partial(show_state, mesh_name="mlp")
 
 
 def attend(query, fresh, window, tails, plen, tlen):
@@ -108,7 +117,7 @@
     every = lax.all_gather(attn, "mlp", axis=2, tiled=True)
     block = lax.dynamic_slice_in_dim(every, position * block_width, block_width, 4)
     partial_sum = jnp.dot(block.reshape(-1, block_width), w_out, preferred_element_type=jnp.float32)
-    mixed = lax.psum(partial_sum, "mlp")
+    mixed = region_match(partial_sum)
     res_all = lax.all_gather(residual, "mlp", axis=2, tiled=True).reshape(-1, width)
     h1_all = (res_all.astype(jnp.float32) + mixed).astype(jnp.bfloat16)
     h1_own = lax.dynamic_slice_in_dim(

time: 240 us -> 208 us (0.87)
  waiting for transfers between devices: 87.3 us -> 49.1 us
  other arithmetic: 33.8 us -> 40.1 us
    psum x1 -> x0, waiting for transfers between devices: 44.4 us -> none  [on_device(): mixed = lax.psum(partial_sum, 'mlp')]
    all_gather x0 -> x1, waiting for transfers between devices: none -> 6.96 us  [show_state(): last = lax.all_gather(mine, axis_name=mesh_name).sum(axis=0)]
    reduce_sum x0 -> x2, local copies, waits for them, and re-layouts: none -> 3.91 us  [show_state(): last = lax.all_gather(mine, axis_name=mesh_name).sum(axis=0)]
    unnamed x56 -> x52, local copies, waits for them, and re-layouts: 8.28 us -> 4.43 us
    reduce_sum x0 -> x2, other arithmetic: none -> 3.34 us  [the longest x1 2.3 us: show_state(): last = lax.all_gather(mine, axis_name=mesh_name).sum(axis=0)]
    convert_element_type x0 -> x2, other arithmetic: none -> 3.02 us  [the longest x1 1.8 us: on_device(): h1_all = (res_all.astype(jnp.float32) + mixed).astype(jnp.bfloat16)]
  transfers between devices with their start and end apart: 3 -> 3, of which waited for: 2 -> 2; matrix products, arithmetic and copies ran while one was open for 17% -> 19% of each run, Pallas kernels for 0% -> 0%
where the time goes in v1:
time: 208 us; the launch traced here: 206 us
  waiting for transfers between devices  49.1 us (24%)
  other arithmetic  40.1 us (19%)
  local copies, waits for them, and re-layouts  34.2 us (16%)
  matrix products  27.6 us (13%)
  blocking collectives  26.4 us (13%)
  between operations  16.2 us (8%)
  starting transfers between devices  12.4 us (6%)
    unnamed x3, waiting for transfers between devices  42.1 us
    all_gather x1, blocking collectives, on_device(): lax.all_gather(residual, 'mlp', axis=2, tiled=True).reshape(-1, width)  13.8 us
    all_gather x1, blocking collectives, on_device(): every = lax.all_gather(attn, 'mlp', axis=2, tiled=True)  12.6 us
    all_to_all x1, starting transfers between devices, on_device(): lax.all_to_all(outgoing, 'req', split_axis=0, concat_axis=0, tiled=True)  12.3 us
    all_gather x1, waiting for transfers between devices, show_state(): last = lax.all_gather(mine, axis_name=mesh_name).sum(axis=0)  6.96 us
    unnamed x52, local copies, waits for them, and re-layouts  4.43 us
    dot_general x1, matrix products, on_device(): jnp.dot(act, w_down, preferred_element_type=jnp.float32)  4.17 us
  transfers between devices with their start and end apart: 3, of which 2 were waited for; matrix products, arithmetic and copies ran while one was open for 19% of the time, Pallas kernels for 0%

profile of v1, /device:TPU:8, one launch (start us, length us, event | category | flops | bytes accessed | tf_op | source)
XLA Modules:
  0.0 206.1 jit_solution(3830413536377131169)
XLA Ops:
  7.2 0.8 compare_select_fusion.1
  8.0 0.8 compare_and_fusion.3
  8.8 3.8 %gather_fusion = bf16[64,20,256]{2,0,1:T(8,128)(2,1)} fusion(bf16[64,20,256]{2,0,1:T(8,128)(2,1)} %param.24, s32[1024]{0:T(1024)S(1)} %pad_clamp_fusion.1), kind=kCustom, calls=%fused_computation.clone | custom fusion | bytes 1310976 | tf_op jit(solution)/shard_map/jit(_take)/gather | solution.py:97
  12.6 1.3 broadcast_select_fusion.1
  13.9 1.3 copy.22
  15.1 12.3 %all-to-all-start = ((bf16[64,20,256]{2,1,0:T(8,128)(2,1)}), bf16[64,20,256]{2,1,0:T(8,128)(2,1)}, u32[]{:S(2)}, u32[]{:S(2)}) async-start(bf16[64,20,256]{2,1,0:T(8,128)(2,1)} %copy.22), calls=%async_computation | async-start | bytes 1572864 | tf_op jit(solution)/shard_map/all_to_all | solution.py:98
  29.4 1.2 compare_select_fusion
  30.6 1.4 fusion.57
  32.0 1.4 fusion.60
  33.9 1.4 reshape_squeeze.6
  36.6 1.6 fusion.63
  38.2 1.5 fusion.61
  39.8 0.8 compare_and_fusion.1
  40.6 2.0 fusion.62
  43.8 1.4 reshape_squeeze.7
  45.1 1.2 pad_clamp_fusion
  46.3 1.6 fusion.30
  48.0 1.9 fusion.11
  49.8 1.1 compare_and_fusion.2
  51.0 0.7 iota_add_fusion
  51.7 1.4 compare_and_fusion
  53.1 2.1 %fusion.64 = (f32[4,2,12]{2,1,0:T(2,128)}, f32[4,2,12,2]{2,3,1,0:T(2,128)}) fusion(bf16[4,2,12,128]{3,2,1,0:T(8,128)(2,1)} %reshape_squeeze.7, bf16[4,2,256]{2,1,0:T(2,128)(2,1)} %get-tuple-element.10, pred[2,2]{1,0:T(4,128)(4,1)} %iota_compare_fusion.8), kind=kOutput, calls=%fused_computation.152 | convolution fusion | flops 49632 | bytes 36480 | tf_op jit(solution)/shard_map/sthd,sud->sthu/dot_general | solution.py:29
  55.2 2.8 %gather_fusion.1 = bf16[64,20,256]{2,1,0:T(8,128)(2,1)} fusion(bf16[64,20,256]{2,1,0:T(8,128)(2,1)} %all-to-all-done, s32[1024]{0:T(1024)} %pad_clamp_fusion), kind=kCustom, calls=%fused_computation.1.clone | custom fusion | bytes 1310976 | tf_op jit(solution)/shard_map/jit(_take)/gather | solution.py:99
  58.0 2.2 %broadcast_select_fusion = bf16[64,20,256]{2,1,0:T(8,128)(2,1)} fusion(bf16[64,20,256]{2,1,0:T(8,128)(2,1)} %gather_fusion.1, pred[64]{0:T(512)(128)(4,1)} %compare_and_fusion.2), kind=kLoop, calls=%fused_computation.25 | loop fusion | flops 327680 | bytes 1310784 | tf_op jit(solution)/shard_map/jit(_take)/select_n | solution.py:99
  60.2 2.0 reshape.397
  62.2 1.0 slice.118
  63.2 2.1 fusion.65
  65.3 1.5 fusion.66
  68.1 1.4 fusion.44
  69.5 0.7 add_add_fusion.1
  70.2 1.4 fusion.22
  71.9 0.9 fusion.7
  72.8 1.4 convert_element_type.101
  74.2 1.0 fusion.31
  75.2 1.3 fusion.12
  76.5 0.7 add_add_fusion
  77.2 1.4 fusion.21
  78.7 1.1 convolution_add_fusion.1
  79.8 1.6 fusion.8
  81.4 1.4 convert_element_type.106
  82.8 0.8 pad_maximum_fusion
  83.6 12.6 %all-gather = bf16[2,16,2,1536]{3,2,1,0:T(2,128)(2,1)S(1)} all-gather(bf16[2,4,2,1536]{3,2,1,0:T(2,128)(2,1)S(1)} %pad_maximum_fusion), channel_id=2, replica_groups=mesh['req'=64,'mlp'=4] {'mlp'}, dimensions={1}, use_global_device_ids=true | all-gather | bytes 245760 | tf_op jit(solution)/shard_map/all_gather | solution.py:117
  96.9 1.4 reshape.399
  98.3 2.4 %fusion.67 = f32[64,1536]{1,0:T(8,128)} fusion(bf16[64,384]{1,0:T(8,128)(2,1)} %reshape.399, bf16[384,1536]{1,0:T(8,128)(2,1)} %param.29), kind=kOutput, calls=%fused_computation.155 | convolution fusion | flops 75497472 | bytes 1622016 | tf_op jit(solution)/shard_map/dot_general | solution.py:119
  100.8 13.8 %all_gather.12 = bf16[1,2,16,2,1536]{4,3,2,1,0:T(2,128)(2,1)} all-gather(bf16[1,2,4,2,1536]{4,3,2,1,0:T(2,128)(2,1)} %param.21), channel_id=1, replica_groups=mesh['req'=64,'mlp'=4] {'mlp'}, dimensions={2}, use_global_device_ids=true | all-gather | bytes 245760 | tf_op jit(solution)/shard_map/all_gather | solution.py:121
  114.6 1.7 reshape.402
  117.5 1.3 dynamic-slice.1
  120.1 1.7 select_select_fusion.1
  121.8 1.8 convert_bitcast_fusion
  123.6 7.0 %all-gather.4.cloned.1.call-done = f32[256,1536]{1,0:T(8,128)} async-done(((f32[64,1536]{1,0:T(8,128)}), f32[256,1536]{1,0:T(8,128)}) %all-gather.4.cloned.1.call-update) | async-done | bytes 1572880 | tf_op jit(solution)/shard_map/all_gather | solution.py:9
  130.6 2.3 %reduce_sum.100 = f32[64,1536]{1,0:T(8,128)} reduce(f32[4,64,1536]{2,1,0:T(8,128)} %bitcast.156, f32[]{:T(128)} %constant.6.clone.1), dimensions={0}, to_apply=%region_12.14 | reduce | flops 294912 | bytes 1966084 | tf_op jit(solution)/shard_map/reduce_sum | solution.py:9
  132.9 2.0 reduce_sum.102
  134.8 1.4 multiply_reduce_fusion
  136.8 1.2 multiply_convert_fusion
  138.7 3.4 %fusion.68 = f32[64,1152]{1,0:T(8,128)} fusion(bf16[64,1536]{1,0:T(8,128)(2,1)S(1)} %multiply_convert_fusion, bf16[1536,1152]{1,0:T(8,128)(2,1)} %param.31), kind=kOutput, calls=%fused_computation.156 | convolution fusion | flops 226492416 | bytes 4030464 | tf_op jit(solution)/shard_map/dot_general | solution.py:127
  142.2 4.2 %convolution_convert_fusion = bf16[64,1536]{1,0:T(8,128)(2,1)} fusion(bf16[1152,1536]{1,0:T(8,128)(2,1)S(1)} %copy-done, bf16[64,1536]{1,0:T(8,128)(2,1)} %copy-done.1, bf16[1536,1152]{1,0:T(8,128)(2,1)} %param.32, f32[64,1152]{1,0:T(8,128)} %fusion.68), kind=kOutput, calls=%fused_computation.4 | convolution fusion | flops 453820416 | bytes 7766016 | tf_op jit(solution)/shard_map/dot_general | solution.py:130
  146.4 1.7 convert_element_type.119
  148.1 1.0 select_select_fusion
  149.1 1.6 maximum_bitcast_fusion
  150.8 2.0 reduce_sum.101
  152.7 42.1 %all-reduce.3.cloned.1.call-done = bf16[2,16,2,1536]{3,2,1,0:T(2,128)(2,1)} async-done(((bf16[2,16,2,1536]{3,2,1,0:T(2,128)(2,1)}), bf16[2,16,2,1536]{3,2,1,0:T(2,128)(2,1)}) %all-reduce.3.cloned.1.call-update) | async-done | bytes 196624
  194.9 1.7 fusion.33
  196.5 1.0 multiply_reduce_fusion.2
  197.5 1.0 multiply_reduce_fusion.1
  (74 shorter events, 9.8 us)
Async XLA Ops:
  7.2 135.0 %copy-start = (bf16[1152,1536]{1,0:T(8,128)(2,1)S(1)}, bf16[1152,1536]{1,0:T(8,128)(2,1)}, u32[]{:S(2)}) copy-start(bf16[1152,1536]{1,0:T(8,128)(2,1)} %param.33) | copy-start | bytes 10616836
  12.6 15.5 %copy-start.20 = (s32[1,2,4]{2,1,0:T(2,128)S(1)}, s32[1,2,4]{2,1,0:T(2,128)}, u32[]{:S(2)}) copy-start(s32[1,2,4]{2,1,0:T(2,128)} %param.28) | copy-start | bytes 100
  12.6 20.7 %copy-start.14 = (bf16[1,2,4,2,256]{4,3,2,1,0:T(2,128)(2,1)S(1)}, bf16[1,2,4,2,256]{4,3,2,1,0:T(2,128)(2,1)}, u32[]{:S(2)}) copy-start(bf16[1,2,4,2,256]{4,3,2,1,0:T(2,128)(2,1)} %param.20) | copy-start | bytes 24580
  15.1 40.1 %all-to-all-start = ((bf16[64,20,256]{2,1,0:T(8,128)(2,1)}), bf16[64,20,256]{2,1,0:T(8,128)(2,1)}, u32[]{:S(2)}, u32[]{:S(2)}) async-start(bf16[64,20,256]{2,1,0:T(8,128)(2,1)} %copy.22), calls=%async_computation | async-start | bytes 1572864 | tf_op jit(solution)/shard_map/all_to_all | solution.py:98
  27.4 103.1 %all-gather.4.cloned.1.call-start = ((), (), s32[]{:S(2)}) async-start(), calls=%async_computation.1 | async-start | bytes 1966080 | tf_op jit(solution)/shard_map/all_gather | solution.py:9
  28.1 5.9 %copy-start.19 = (s32[4]{0:T(128)}, s32[4]{0:T(128)S(1)}, u32[]{:S(2)}) copy-start(s32[4]{0:T(128)S(1)} %get-tuple-element.19) | copy-start | bytes 52
  29.4 8.8 %copy-start.17 = (pred[4,64]{1,0:T(4,128)(4,1)}, pred[4,64]{1,0:T(4,128)(4,1)S(1)}, u32[]{:S(2)}) copy-start(pred[4,64]{1,0:T(4,128)(4,1)S(1)} %get-tuple-element.38) | copy-start | bytes 772
  33.9 4.3 %copy-start.9 = (bf16[4,2,256]{2,1,0:T(2,128)(2,1)}, bf16[4,2,256]{2,1,0:T(2,128)(2,1)S(1)}, u32[]{:S(2)}) copy-start(bf16[4,2,256]{2,1,0:T(2,128)(2,1)S(1)} %get-tuple-element.11) | copy-start | bytes 12292
  62.2 9.4 %copy-start.3 = (bf16[1,4,64,256]{3,2,1,0:T(8,128)(2,1)S(1)}, bf16[1,4,64,256]{3,2,1,0:T(8,128)(2,1)}, u32[]{:S(2)}) copy-start(bf16[1,4,64,256]{3,2,1,0:T(8,128)(2,1)} %param.23) | copy-start | bytes 393220
  62.2 9.5 %copy-start.4 = (f32[4,2,12,64]{3,2,1,0:T(8,128)S(1)}, f32[4,2,12,64]{3,2,1,0:T(8,128)}, u32[]{:S(2)}) copy-start(f32[4,2,12,64]{3,2,1,0:T(8,128)} %get-tuple-element.31) | copy-start | bytes 73732
  62.2 9.5 %copy-start.5 = (f32[1,8,12]{2,1,0:T(8,128)S(1)}, f32[1,8,12]{2,1,0:T(8,128)}, u32[]{:S(2)}) copy-start(f32[1,8,12]{2,1,0:T(8,128)} %maximum_maximum_fusion.1) | copy-start | bytes 1156
  62.2 9.5 %copy-start.18 = (pred[4,64]{1,0:T(4,128)(4,1)S(1)}, pred[4,64]{1,0:T(4,128)(4,1)}, u32[]{:S(2)}) copy-start(pred[4,64]{1,0:T(4,128)(4,1)} %copy-done.17) | copy-start | bytes 772
  62.2 9.7 %copy-start.10 = (bf16[4,2,256]{2,1,0:T(2,128)(2,1)S(1)}, bf16[4,2,256]{2,1,0:T(2,128)(2,1)}, u32[]{:S(2)}) copy-start(bf16[4,2,256]{2,1,0:T(2,128)(2,1)} %copy-done.9) | copy-start | bytes 12292
  62.2 9.7 %copy-start.15 = (f32[4,2,12,2]{2,3,1,0:T(2,128)S(1)}, f32[4,2,12,2]{2,3,1,0:T(2,128)}, u32[]{:S(2)}) copy-start(f32[4,2,12,2]{2,3,1,0:T(2,128)} %get-tuple-element.27) | copy-start | bytes 2308
  62.2 9.7 %copy-start.22 = (pred[2,2]{1,0:T(4,128)(4,1)S(1)}, pred[2,2]{1,0:T(4,128)(4,1)}, u32[]{:S(2)}) copy-start(pred[2,2]{1,0:T(4,128)(4,1)} %iota_compare_fusion.8) | copy-start | bytes 16
  63.2 2.1 %copy-start.2 = (bf16[256,256]{1,0:T(8,128)(2,1)}, bf16[256,256]{1,0:T(8,128)(2,1)S(1)}, u32[]{:S(2)}) copy-start(bf16[256,256]{1,0:T(8,128)(2,1)S(1)} %slice.118) | copy-start | bytes 393220
  67.5 0.6 copy-start.6
  71.6 7.0 %copy-start.7 = (f32[1,8,12]{2,1,0:T(8,128)S(1)}, f32[1,8,12]{2,1,0:T(8,128)}, u32[]{:S(2)}) copy-start(f32[1,8,12]{2,1,0:T(8,128)} %copy-done.6) | copy-start | bytes 1156
  71.7 8.1 %copy-start.8 = (bf16[4,2,256]{2,1,0:T(2,128)(2,1)S(1)}, bf16[4,2,256]{2,1,0:T(2,128)(2,1)}, u32[]{:S(2)}) copy-start(bf16[4,2,256]{2,1,0:T(2,128)(2,1)} %get-tuple-element.10) | copy-start | bytes 12292
  76.5 39.8 %copy-start.11 = (bf16[4,2,256]{2,1,0:T(2,128)(2,1)S(1)}, bf16[4,2,256]{2,1,0:T(2,128)(2,1)}, u32[]{:S(2)}) copy-start(bf16[4,2,256]{2,1,0:T(2,128)(2,1)} %copy-done.9) | copy-start | bytes 12292
  76.5 42.9 %copy-start.21 = (s32[1,2,4]{2,1,0:T(2,128)S(1)}, s32[1,2,4]{2,1,0:T(2,128)}, u32[]{:S(2)}) copy-start(s32[1,2,4]{2,1,0:T(2,128)} %param.28) | copy-start | bytes 100
  100.7 94.1 %all-reduce.3.cloned.1.call-start = ((), (), s32[]{:S(2)}) async-start(), calls=%async_computation.2 | async-start | bytes 393216
  138.1 0.7 copy-start.1
  142.2 5.9 %copy-start.12 = (bf16[4,1,256]{2,0,1:T(4,128)(2,1)S(1)}, bf16[4,1,256]{2,0,1:T(4,128)(2,1)}, u32[]{:S(2)}) copy-start(bf16[4,1,256]{2,0,1:T(4,128)(2,1)} %copy.46) | copy-start | bytes 6148
  142.2 5.9 %copy-start.13 = (bf16[4,1,256]{2,0,1:T(4,128)(2,1)S(1)}, bf16[4,1,256]{2,0,1:T(4,128)(2,1)}, u32[]{:S(2)}) copy-start(bf16[4,1,256]{2,0,1:T(4,128)(2,1)} %copy.47) | copy-start | bytes 6148
  142.2 55.3 %copy-start.16 = (f32[1536]{0:T(1024)S(1)}, f32[1536]{0:T(1024)}, u32[]{:S(2)}) copy-start(f32[1536]{0:T(1024)} %param.35) | copy-start | bytes 18436
Sparse Core Ops, SparseCore 0:
  100.9 29.6 all-gather.3
  148.2 46.6 all-reduce.2
